TPU v7x, 32 devices: a whole 2x2x4 slice. The times are simulated.
32 devices in a mesh: ia: 4 (over y, x), ja: 2 (over core), ka: 4 (over z).
Axes of the slice: x: 2, y: 2, z: 4, core: 2. Of those that a mesh axis runs over, the one named last changes fastest.
Arguments:
- tensor: bfloat16 [128, 256, 1024], P('ia', 'ja', 'ka'), may hold values from 5 to 200
- factor_first: bfloat16 [128, 256], P('ia', ('ja', 'ka')), may hold values from 0.19921875 to 1.5
- factor_second: bfloat16 [256, 256], P('ja', ('ia', 'ka')), may hold values from 0.19921875 to 1.5
- factor_third: bfloat16 [1024, 256], P('ka', ('ia', 'ja')), may hold values from 0.19921875 to 1.5
Outputs:
- grad_first: float32 [128, 256], P('ia', ('ja', 'ka'))
- grad_second: float32 [256, 256], P('ja', ('ia', 'ka'))
- grad_third: float32 [1024, 256], P('ka', ('ia', 'ja'))
All inputs are finite; a program needn't handle non-finite values.
Results may differ from a plain program's by a relative error of at most 0.005.
Values may be sent and summed in bfloat16 or wider, within the bound.
No kernel may reach another device: no remote copies, remote signals or barrier semaphores. Data moves between devices by JAX's collectives and lax.ppermute only.
A program may use at most 64 MiB of HBM per device.

v0:
```python
import jax
import jax.numpy as jnp
from jax import lax
from jax.sharding import PartitionSpec as P


def body(tensor, factor_first, factor_second, factor_third):
    full_first = lax.all_gather(factor_first, ("ja", "ka"), axis=1, tiled=True)
    full_second = lax.all_gather(factor_second, ("ia", "ka"), axis=1, tiled=True)
    full_third = lax.all_gather(factor_third, ("ia", "ja"), axis=1, tiled=True)
    rows_i, rows_j, rows_k = tensor.shape
    rank = full_first.shape[1]
    total_i = rows_i * lax.axis_size("ia")
    total_j = rows_j * lax.axis_size("ja")
    total_k = rows_k * lax.axis_size("ka")
    first32 = full_first.astype(jnp.float32)
    second32 = full_second.astype(jnp.float32)
    khatri = (first32[:, None, :] * second32[None, :, :]).astype(jnp.bfloat16)
    khatri_flat = khatri.reshape(rows_i * rows_j, rank)
    model = jnp.einsum("mr,kr->mk", khatri_flat, full_third, preferred_element_type=jnp.float32)
    flat_data = tensor.reshape(rows_i * rows_j, rows_k).astype(jnp.float32)
    deriv = ((model - flat_data) * lax.rsqrt(model)).astype(jnp.bfloat16)
    part_third = jnp.einsum("mk,mr->kr", deriv, khatri_flat, preferred_element_type=jnp.float32)
    inner = jnp.einsum("mk,kr->mr", deriv, full_third, preferred_element_type=jnp.float32)
    inner = inner.reshape(rows_i, rows_j, rank)
    part_first = jnp.sum(inner * second32[None, :, :], axis=1) / (total_j * total_k)
    part_second = jnp.sum(inner * first32[:, None, :], axis=0) / (total_i * total_k)
    part_third = part_third / (total_i * total_j)
    grad_first = lax.psum_scatter(part_first, ("ja", "ka"), scatter_dimension=1, tiled=True)
    grad_second = lax.psum_scatter(part_second, ("ia", "ka"), scatter_dimension=1, tiled=True)
    grad_third = lax.psum_scatter(part_third, ("ia", "ja"), scatter_dimension=1, tiled=True)
    return (grad_first, grad_second, grad_third)


def solution(mesh):
    placed = (
        P("ia", "ja", "ka"),
        P("ia", ("ja", "ka")),
        P("ja", ("ia", "ka")),
        P("ka", ("ia", "ja")),
    )
    return jax.shard_map(
        body,
        mesh=mesh,
        in_specs=placed,
        out_specs=(P("ia", ("ja", "ka")), P("ja", ("ia", "ka")), P("ka", ("ia", "ja"))),
        check_vma=False,
    )
```

profile of v0, /device:TPU:0, one launch (start us, length us, event | category | flops | bytes accessed | tf_op | source)
XLA Modules:
  0.0 234.9 jit_solution(1074803909325882737)
XLA Ops:
  7.2 0.0 reduce-scatter.10.cloned.1.call-start
  7.2 0.8 copy.16
  8.0 25.6 %all_gather.9 = bf16[32,256]{0,1:T(8,128)(2,1)S(1)} all-gather(bf16[32,32]{0,1:T(8,128)(2,1)S(1)} %copy.16), channel_id=1, replica_groups=mesh['ia'=4,'ja'=2,'ka'=4] {'ja','ka'}, dimensions={1}, use_global_device_ids=true | all-gather | bytes 18432 | tf_op jit(solution)/shard_map/all_gather | solution.py:8
  33.6 0.1 copy.17
  33.7 41.3 %all_gather.10 = bf16[128,256]{0,1:T(8,128)(2,1)S(1)} all-gather(bf16[128,16]{0,1:T(8,128)(2,1)} %param.6), channel_id=1, replica_groups=mesh['ia'=4,'ja'=2,'ka'=4] {'ia','ka'}, dimensions={1}, use_global_device_ids=true | all-gather | bytes 69632 | tf_op jit(solution)/shard_map/all_gather | solution.py:9
  75.0 0.1 copy.18
  75.1 0.0 copy-start.1
  75.1 8.5 %all_gather.11 = bf16[256,256]{0,1:T(8,128)(2,1)S(1)} all-gather(bf16[256,32]{0,1:T(8,128)(2,1)} %param.7), channel_id=1, replica_groups=mesh['ia'=4,'ja'=2,'ka'=4] {'ia','ja'}, dimensions={1}, use_global_device_ids=true | all-gather | bytes 147456 | tf_op jit(solution)/shard_map/all_gather | solution.py:10
  83.6 0.6 multiply_convert_fusion
  84.3 0.0 copy-start
  84.3 0.0 copy-done.1
  84.3 0.9 fusion.1
  85.2 0.4 copy-done
  85.6 2.7 %multiply_reduce_fusion.1 = (f32[32,256]{1,0:T(8,128)S(1)}, f32[4096,256]{1,0:T(8,128)}) fusion(f32[128,256]{1,0:T(8,128)S(1)} %copy.18, bf16[4096,256]{1,0:T(8,128)(2,1)S(1)} %fusion.1, bf16[256,256]{0,1:T(8,128)(2,1)S(1)} %all_gather.11), kind=kOutput, calls=%fused_computation.4 | convolution fusion | flops 538959872 | bytes 6586368 | tf_op jit(solution)/shard_map/mk,kr->mr/dot_general | solution.py:24
  88.3 0.7 copy.20
  89.0 0.0 reduce-scatter.10.cloned.1.call-update
  89.0 0.0 reduce-scatter.12.cloned.1.call-start
  89.1 2.6 %multiply_reduce_fusion = f32[128,256]{1,0:T(8,128)S(1)} fusion(f32[32,128,256]{2,1,0:T(8,128)} %bitcast.16, f32[32,256]{1,0:T(8,128)S(1)} %convert_element_type.22), kind=kLoop, calls=%fused_computation.3 | loop fusion | flops 2064384 | bytes 4358144 | tf_op jit(solution)/shard_map/reduce_sum | solution.py:27
  91.7 0.8 copy.22
  92.4 0.0 reduce-scatter.12.cloned.1.call-update
  92.5 0.0 reduce-scatter.8.cloned.1.call-start
  92.5 3.2 %convolution_multiply_fusion = f32[256,256]{0,1:T(8,128)} fusion(bf16[4096,256]{1,0:T(8,128)(2,1)S(1)} %fusion.1, bf16[4096,256]{1,0:T(8,128)(2,1)} %bitcast.18), kind=kOutput, calls=%fused_computation.6 | convolution fusion | flops 536936448 | bytes 4456448 | tf_op jit(solution)/shard_map/mk,mr->kr/dot_general | solution.py:23
  95.7 0.0 reduce-scatter.8.cloned.1.call-update
  95.7 21.5 %reduce-scatter.10.cloned.1.call-done = f32[32,32]{1,0:T(8,128)} async-done(((f32[256,32]{1,0:T(8,128)}), f32[32,32]{1,0:T(8,128)}) %reduce-scatter.10.cloned.1.call-update) | async-done | bytes 4112
  117.3 1.4 copy.21
  118.7 75.9 %reduce-scatter.12.cloned.1.call-done = f32[16,128]{1,0:T(8,128)} async-done(((f32[256,128]{1,0:T(8,128)}), f32[16,128]{1,0:T(8,128)}) %reduce-scatter.12.cloned.1.call-update) | async-done | bytes 8208
  194.6 33.8 %reduce-scatter.8.cloned.1.call-done = f32[256,32]{0,1:T(8,128)} async-done(((f32[256,256]{0,1:T(8,128)}), f32[256,32]{0,1:T(8,128)}) %reduce-scatter.8.cloned.1.call-update) | async-done | bytes 32784 | tf_op jit(solution)/shard_map/reduce_scatter | solution.py:31
  (3 shorter events, 0.0 us)
Async XLA Ops:
  7.2 110.1 %reduce-scatter.10.cloned.1.call-start = ((), (), s32[]{:S(2)}) async-start(), calls=%async_computation.4 | async-start | bytes 147456
  75.1 9.2 %copy-start.1 = (bf16[32,128,256]{2,1,0:T(8,128)(2,1)S(1)}, bf16[32,128,256]{2,1,0:T(8,128)(2,1)}, u32[]{:S(2)}) copy-start(bf16[32,128,256]{2,1,0:T(8,128)(2,1)} %param.4) | copy-start | bytes 6291460
  84.3 1.3 copy-start
  89.0 105.6 %reduce-scatter.12.cloned.1.call-start = ((), (), s32[]{:S(2)}) async-start(), calls=%async_computation.5 | async-start | bytes 139264
  92.5 136.0 %reduce-scatter.8.cloned.1.call-start = ((), (), s32[]{:S(2)}) async-start(), calls=%async_computation.3 | async-start | bytes 294912 | tf_op jit(solution)/shard_map/reduce_scatter | solution.py:31
Sparse Core Ops, SparseCore 0:
  89.2 28.0 reduce-scatter.9
  120.2 74.3 reduce-scatter.11
  198.2 30.1 reduce-scatter.7
where the time goes:
time: 235 us
  waiting for transfers between devices  131 us (56%)
  blocking collectives  75.4 us (32%)
  between operations  13.8 us (6%)
  matrix products  6.78 us (3%)
  local copies, waits for them, and re-layouts  4.27 us (2%)
  other arithmetic  3.22 us (1%)
    unnamed x5, waiting for transfers between devices  97.5 us
    all_gather x1, blocking collectives, body(): lax.all_gather(factor_second, ('ia', 'ka'), axis=1, tiled=True)  41.3 us
    reduce_scatter x1, waiting for transfers between devices, body(): lax.psum_scatter(part_third, ('ia', 'ja'), scatter_dimension=1, tiled=True)  33.8 us
    all_gather x1, blocking collectives, body(): full_first = lax.all_gather(factor_first, ('ja', 'ka'), axis=1, tiled=True)  25.6 us
    all_gather x1, blocking collectives, body(): full_third = lax.all_gather(factor_third, ('ia', 'ja'), axis=1, tiled=True)  8.54 us
  transfers between devices with their start and end apart: 3, of which 3 were waited for; matrix products, arithmetic and copies ran while one was open for 3% of the time, Pallas kernels for 0%

commit v1 on v0

--- a/solution.py
+++ b/solution.py
@@ -4,9 +4,37 @@
 from jax.sharding import PartitionSpec as P
 
 
+def _expand_column(mine, dim_no):
+    work_now = jax.lax.axis_size(("ia", "ka"))
+    r1, r_now, mixed_arr = (work_now, jax.lax.axis_index(("ia", "ka")), mine.shape[dim_no])
+    slots = []
+    i = 0
+    while i < r1:
+        slots.append((i, (i + 1) % r1))
+        i = i + 1
+    tray = []
+    i = 0
+    while i < r1:
+        tray.append((i, (i - 1) % r1))
+        i = i + 1
+    z = jnp.zeros((*mine.shape[:dim_no], r1 * mixed_arr, *mine.shape[dim_no + 1 :]), mine.dtype)
+    z = lax.dynamic_update_slice_in_dim(z, mine, r_now * mixed_arr, axis=dim_no)
+    formed = now = mine
+    out_arr = r1 // 2
+    nth = 1
+    while nth < out_arr + 1:
+        formed = jax.lax.ppermute(formed, ("ia", "ka"), slots)
+        z = lax.dynamic_update_slice_in_dim(z, formed, (r_now - nth) % r1 * mixed_arr, axis=dim_no)
+        if nth < r1 - out_arr:
+            now = jax.lax.ppermute(now, ("ia", "ka"), tray)
+            z = lax.dynamic_update_slice_in_dim(z, now, (r_now + nth) % r1 * mixed_arr, axis=dim_no)
+        nth += 1
+    return z
+
+
 def body(tensor, factor_first, factor_second, factor_third):
     full_first = lax.all_gather(factor_first, ("ja", "ka"), axis=1, tiled=True)
-    full_second = lax.all_gather(factor_second, ("ia", "ka"), axis=1, tiled=True)
+    full_second = _expand_column(factor_second, 1)
     full_third = lax.all_gather(factor_third, ("ia", "ja"), axis=1, tiled=True)
     rows_i, rows_j, rows_k = tensor.shape
     rank = full_first.shape[1]

time: 235 us -> 255 us (1.085)
  blocking collectives: 75.4 us -> 33.1 us
  starting transfers between devices: 0.12 us -> 41.5 us
  waiting for transfers between devices: 131 us -> 145 us
  local copies, waits for them, and re-layouts: 4.27 us -> 13.9 us
    ppermute x0 -> x15, starting transfers between devices: none -> 41.4 us  [the longest x7 38.3 us: _expand_column(): now = jax.lax.ppermute(now, ('ia', 'ka'), tray)]
    all_gather x1 -> x0, blocking collectives: 41.3 us -> none  [body(): lax.all_gather(factor_second, ('ia', 'ka'), axis=1, tiled=True)]
    ppermute x0 -> x15, waiting for transfers between devices: none -> 6.78 us  [the longest x8 4.9 us: _expand_column(): formed = jax.lax.ppermute(formed, ('ia', 'ka'), slots)]
    unnamed x5, waiting for transfers between devices: 97.5 us -> 104 us
    dynamic_update_slice x0 -> x16, local copies, waits for them, and re-layouts: none -> 6.22 us  [the longest x7 3 us: _expand_column(): lax.dynamic_update_slice_in_dim(z, now, (r_now + nth) % r1 * mixed_arr, a...]
    unnamed x8 -> x7, local copies, waits for them, and re-layouts: 4.1 us -> 5.78 us
  transfers between devices with their start and end apart: 3 -> 18, of which waited for: 3 -> 8; matrix products, arithmetic and copies ran while one was open for 3% -> 6% of each run, Pallas kernels for 0% -> 0%
where the time goes in v1:
time: 255 us
  waiting for transfers between devices  145 us (57%)
  starting transfers between devices  41.5 us (16%)
  blocking collectives  33.1 us (13%)
  between operations  14.1 us (6%)
  local copies, waits for them, and re-layouts  13.9 us (5%)
  matrix products  6.4 us (3%)
    unnamed x5, waiting for transfers between devices  104 us
    ppermute x7, starting transfers between devices, _expand_column(): now = jax.lax.ppermute(now, ('ia', 'ka'), tray)  38.3 us
    reduce_scatter x1, waiting for transfers between devices, body(): lax.psum_scatter(part_third, ('ia', 'ja'), scatter_dimension=1, tiled=True)  33.6 us
    all_gather x1, blocking collectives, body(): full_first = lax.all_gather(factor_first, ('ja', 'ka'), axis=1, tiled=True)  23.8 us
    all_gather x1, blocking collectives, body(): full_third = lax.all_gather(factor_third, ('ia', 'ja'), axis=1, tiled=True)  9.31 us
    unnamed x7, local copies, waits for them, and re-layouts  5.78 us
  transfers between devices with their start and end apart: 18, of which 8 were waited for; matrix products, arithmetic and copies ran while one was open for 6% of the time, Pallas kernels for 0%

profile of v1, /device:TPU:0, one launch (start us, length us, event | category | flops | bytes accessed | tf_op | source)
XLA Modules:
  0.0 254.8 jit_solution(17053710485362711936)
XLA Ops:
  7.2 3.1 %collective-permute-start = (bf16[128,16]{0,1:T(8,128)(2,1)}, bf16[128,16]{0,1:T(8,128)(2,1)S(1)}, u32[]{:S(2)}, u32[]{:S(2)}) collective-permute-start(bf16[128,16]{0,1:T(8,128)(2,1)} %param.6), channel_id=1, source_target_pairs={{0,1},{1,2},{2,3},{3,8},{8,9},{9,10},{10,11},{11,16},{16,17},{17,1... | collective-permute-start | bytes 12296 | tf_op jit(solution)/shard_map/ppermute | solution.py:26
  10.3 4.0 %collective-permute-start.1 = (bf16[128,16]{0,1:T(8,128)(2,1)}, bf16[128,16]{0,1:T(8,128)(2,1)S(1)}, u32[]{:S(2)}, u32[]{:S(2)}) collective-permute-start(bf16[128,16]{0,1:T(8,128)(2,1)} %param.6), channel_id=1, source_target_pairs={{0,27},{1,0},{2,1},{3,2},{8,3},{9,8},{10,9},{11,10},{16,11},{17,16... | collective-permute-start | bytes 12296 | tf_op jit(solution)/shard_map/ppermute | solution.py:29
  14.3 1.8 collective-permute-done
  16.0 5.6 %collective-permute-start.3 = (bf16[128,16]{0,1:T(8,128)(2,1)S(1)}, bf16[128,16]{0,1:T(8,128)(2,1)S(1)}, u32[]{:S(2)}, u32[]{:S(2)}) collective-permute-start(bf16[128,16]{0,1:T(8,128)(2,1)S(1)} %collective-permute-done.1), channel_id=1, source_target_pairs={{0,27},{1,0},{2,1},{3,2},{8,3},{9,8},{10,9},{11,10},{16,11},{17,16... | collective-permute-start | bytes 12296 | tf_op jit(solution)/shard_map/ppermute | solution.py:29
  21.7 1.6 collective-permute-done.2
  23.2 5.6 %collective-permute-start.5 = (bf16[128,16]{0,1:T(8,128)(2,1)S(1)}, bf16[128,16]{0,1:T(8,128)(2,1)S(1)}, u32[]{:S(2)}, u32[]{:S(2)}) collective-permute-start(bf16[128,16]{0,1:T(8,128)(2,1)S(1)} %collective-permute-done.3), channel_id=1, source_target_pairs={{0,27},{1,0},{2,1},{3,2},{8,3},{9,8},{10,9},{11,10},{16,11},{17,16... | collective-permute-start | bytes 12296 | tf_op jit(solution)/shard_map/ppermute | solution.py:29
  28.9 1.6 collective-permute-done.4
  30.4 9.3 %all_gather.7 = bf16[256,256]{0,1:T(8,128)(2,1)S(1)} all-gather(bf16[256,32]{0,1:T(8,128)(2,1)} %param.7), channel_id=1, replica_groups=mesh['ia'=4,'ja'=2,'ka'=4] {'ia','ja'}, dimensions={1}, use_global_device_ids=true | all-gather | bytes 147456 | tf_op jit(solution)/shard_map/all_gather | solution.py:38
  39.7 5.6 %collective-permute-start.7 = (bf16[128,16]{0,1:T(8,128)(2,1)S(1)}, bf16[128,16]{0,1:T(8,128)(2,1)S(1)}, u32[]{:S(2)}, u32[]{:S(2)}) collective-permute-start(bf16[128,16]{0,1:T(8,128)(2,1)S(1)} %collective-permute-done.5), channel_id=1, source_target_pairs={{0,27},{1,0},{2,1},{3,2},{8,3},{9,8},{10,9},{11,10},{16,11},{17,16... | collective-permute-start | bytes 12296 | tf_op jit(solution)/shard_map/ppermute | solution.py:29
  45.4 1.3 collective-permute-done.7
  46.7 5.9 %collective-permute-start.9 = (bf16[128,16]{0,1:T(8,128)(2,1)S(1)}, bf16[128,16]{0,1:T(8,128)(2,1)S(1)}, u32[]{:S(2)}, u32[]{:S(2)}) collective-permute-start(bf16[128,16]{0,1:T(8,128)(2,1)S(1)} %collective-permute-done.7), channel_id=1, source_target_pairs={{0,27},{1,0},{2,1},{3,2},{8,3},{9,8},{10,9},{11,10},{16,11},{17,16... | collective-permute-start | bytes 12296 | tf_op jit(solution)/shard_map/ppermute | solution.py:29
  52.6 0.8 copy.61
  53.4 0.5 collective-permute-done.9
  53.9 5.9 %collective-permute-start.11 = (bf16[128,16]{0,1:T(8,128)(2,1)S(1)}, bf16[128,16]{0,1:T(8,128)(2,1)S(1)}, u32[]{:S(2)}, u32[]{:S(2)}) collective-permute-start(bf16[128,16]{0,1:T(8,128)(2,1)S(1)} %collective-permute-done.9), channel_id=1, source_target_pairs={{0,27},{1,0},{2,1},{3,2},{8,3},{9,8},{10,9},{11,10},{16,11},{17,16... | collective-permute-start | bytes 12296 | tf_op jit(solution)/shard_map/ppermute | solution.py:29
  59.8 23.8 %all_gather.6 = bf16[32,256]{0,1:T(8,128)(2,1)S(1)} all-gather(bf16[32,32]{0,1:T(8,128)(2,1)S(1)} %copy.61), channel_id=1, replica_groups=mesh['ia'=4,'ja'=2,'ka'=4] {'ja','ka'}, dimensions={1}, use_global_device_ids=true | all-gather | bytes 18432 | tf_op jit(solution)/shard_map/all_gather | solution.py:36
  83.6 5.7 %collective-permute-start.13 = (bf16[128,16]{0,1:T(8,128)(2,1)S(1)}, bf16[128,16]{0,1:T(8,128)(2,1)S(1)}, u32[]{:S(2)}, u32[]{:S(2)}) collective-permute-start(bf16[128,16]{0,1:T(8,128)(2,1)S(1)} %collective-permute-done.11), channel_id=1, source_target_pairs={{0,27},{1,0},{2,1},{3,2},{8,3},{9,8},{10,9},{11,10},{16,11},{17,16... | collective-permute-start | bytes 12296 | tf_op jit(solution)/shard_map/ppermute | solution.py:29
  89.3 0.8 copy.63
  91.2 0.4 dynamic_update_slice.50
  92.2 0.4 dynamic_update_slice.52
  93.3 0.4 dynamic_update_slice.54
  98.5 0.6 multiply_convert_fusion
  99.2 1.3 copy-done
  100.5 2.4 fusion.1
  102.9 0.8 multiply_reduce_fusion.1
  103.7 0.5 multiply_reduce_fusion
  104.2 0.7 copy.80
  105.0 0.7 copy.82
  105.8 3.2 %convolution_multiply_fusion = f32[256,256]{0,1:T(8,128)} fusion(bf16[4096,256]{1,0:T(8,128)(2,1)S(1)} %fusion.1, bf16[4096,256]{1,0:T(8,128)(2,1)} %bitcast.18), kind=kOutput, calls=%fused_computation.6 | convolution fusion | flops 536936448 | bytes 4456448 | tf_op jit(solution)/shard_map/mk,mr->kr/dot_general | solution.py:51
  109.1 28.2 %reduce-scatter.10.cloned.1.call-done = f32[32,32]{1,0:T(8,128)} async-done(((f32[256,32]{1,0:T(8,128)}), f32[32,32]{1,0:T(8,128)}) %reduce-scatter.10.cloned.1.call-update) | async-done | bytes 4112
  137.3 1.4 copy.81
  138.6 76.0 %reduce-scatter.12.cloned.1.call-done = f32[16,128]{1,0:T(8,128)} async-done(((f32[256,128]{1,0:T(8,128)}), f32[16,128]{1,0:T(8,128)}) %reduce-scatter.12.cloned.1.call-update) | async-done | bytes 8208
  214.6 33.6 %reduce-scatter.8.cloned.1.call-done = f32[256,32]{0,1:T(8,128)} async-done(((f32[256,256]{0,1:T(8,128)}), f32[256,32]{0,1:T(8,128)}) %reduce-scatter.8.cloned.1.call-update) | async-done | bytes 32784 | tf_op jit(solution)/shard_map/reduce_scatter | solution.py:59
  (58 shorter events, 7.1 us)
Async XLA Ops:
  7.2 130.1 %reduce-scatter.10.cloned.1.call-start = ((), (), s32[]{:S(2)}) async-start(), calls=%async_computation.4 | async-start | bytes 147456
  7.2 8.8 %collective-permute-start = (bf16[128,16]{0,1:T(8,128)(2,1)}, bf16[128,16]{0,1:T(8,128)(2,1)S(1)}, u32[]{:S(2)}, u32[]{:S(2)}) collective-permute-start(bf16[128,16]{0,1:T(8,128)(2,1)} %param.6), channel_id=1, source_target_pairs={{0,1},{1,2},{2,3},{3,8},{8,9},{9,10},{10,11},{11,16},{16,17},{17,1... | collective-permute-start | bytes 12296 | tf_op jit(solution)/shard_map/ppermute | solution.py:26
  10.3 5.8 %collective-permute-start.1 = (bf16[128,16]{0,1:T(8,128)(2,1)}, bf16[128,16]{0,1:T(8,128)(2,1)S(1)}, u32[]{:S(2)}, u32[]{:S(2)}) collective-permute-start(bf16[128,16]{0,1:T(8,128)(2,1)} %param.6), channel_id=1, source_target_pairs={{0,27},{1,0},{2,1},{3,2},{8,3},{9,8},{10,9},{11,10},{16,11},{17,16... | collective-permute-start | bytes 12296 | tf_op jit(solution)/shard_map/ppermute | solution.py:29
  16.0 7.2 %collective-permute-start.2 = (bf16[128,16]{0,1:T(8,128)(2,1)S(1)}, bf16[128,16]{0,1:T(8,128)(2,1)S(1)}, u32[]{:S(2)}, u32[]{:S(2)}) collective-permute-start(bf16[128,16]{0,1:T(8,128)(2,1)S(1)} %collective-permute-done), channel_id=1, source_target_pairs={{0,1},{1,2},{2,3},{3,8},{8,9},{9,10},{10,11},{11,16},{16,17},{17,1... | collective-permute-start | bytes 12296 | tf_op jit(solution)/shard_map/ppermute | solution.py:26
  16.0 7.2 %collective-permute-start.3 = (bf16[128,16]{0,1:T(8,128)(2,1)S(1)}, bf16[128,16]{0,1:T(8,128)(2,1)S(1)}, u32[]{:S(2)}, u32[]{:S(2)}) collective-permute-start(bf16[128,16]{0,1:T(8,128)(2,1)S(1)} %collective-permute-done.1), channel_id=1, source_target_pairs={{0,27},{1,0},{2,1},{3,2},{8,3},{9,8},{10,9},{11,10},{16,11},{17,16... | collective-permute-start | bytes 12296 | tf_op jit(solution)/shard_map/ppermute | solution.py:29
  23.2 7.2 %collective-permute-start.4 = (bf16[128,16]{0,1:T(8,128)(2,1)S(1)}, bf16[128,16]{0,1:T(8,128)(2,1)S(1)}, u32[]{:S(2)}, u32[]{:S(2)}) collective-permute-start(bf16[128,16]{0,1:T(8,128)(2,1)S(1)} %collective-permute-done.2), channel_id=1, source_target_pairs={{0,1},{1,2},{2,3},{3,8},{8,9},{9,10},{10,11},{11,16},{16,17},{17,1... | collective-permute-start | bytes 12296 | tf_op jit(solution)/shard_map/ppermute | solution.py:26
  23.2 16.5 %collective-permute-start.5 = (bf16[128,16]{0,1:T(8,128)(2,1)S(1)}, bf16[128,16]{0,1:T(8,128)(2,1)S(1)}, u32[]{:S(2)}, u32[]{:S(2)}) collective-permute-start(bf16[128,16]{0,1:T(8,128)(2,1)S(1)} %collective-permute-done.3), channel_id=1, source_target_pairs={{0,27},{1,0},{2,1},{3,2},{8,3},{9,8},{10,9},{11,10},{16,11},{17,16... | collective-permute-start | bytes 12296 | tf_op jit(solution)/shard_map/ppermute | solution.py:29
  30.4 15.0 %collective-permute-start.6 = (bf16[128,16]{0,1:T(8,128)(2,1)S(1)}, bf16[128,16]{0,1:T(8,128)(2,1)S(1)}, u32[]{:S(2)}, u32[]{:S(2)}) collective-permute-start(bf16[128,16]{0,1:T(8,128)(2,1)S(1)} %collective-permute-done.4), channel_id=1, source_target_pairs={{0,1},{1,2},{2,3},{3,8},{8,9},{9,10},{10,11},{11,16},{16,17},{17,1... | collective-permute-start | bytes 12296 | tf_op jit(solution)/shard_map/ppermute | solution.py:26
  39.7 7.0 %collective-permute-start.7 = (bf16[128,16]{0,1:T(8,128)(2,1)S(1)}, bf16[128,16]{0,1:T(8,128)(2,1)S(1)}, u32[]{:S(2)}, u32[]{:S(2)}) collective-permute-start(bf16[128,16]{0,1:T(8,128)(2,1)S(1)} %collective-permute-done.5), channel_id=1, source_target_pairs={{0,27},{1,0},{2,1},{3,2},{8,3},{9,8},{10,9},{11,10},{16,11},{17,16... | collective-permute-start | bytes 12296 | tf_op jit(solution)/shard_map/ppermute | solution.py:29
  45.4 7.2 %collective-permute-start.8 = (bf16[128,16]{0,1:T(8,128)(2,1)S(1)}, bf16[128,16]{0,1:T(8,128)(2,1)S(1)}, u32[]{:S(2)}, u32[]{:S(2)}) collective-permute-start(bf16[128,16]{0,1:T(8,128)(2,1)S(1)} %collective-permute-done.6), channel_id=1, source_target_pairs={{0,1},{1,2},{2,3},{3,8},{8,9},{9,10},{10,11},{11,16},{16,17},{17,1... | collective-permute-start | bytes 12296 | tf_op jit(solution)/shard_map/ppermute | solution.py:26
  46.7 7.2 %collective-permute-start.9 = (bf16[128,16]{0,1:T(8,128)(2,1)S(1)}, bf16[128,16]{0,1:T(8,128)(2,1)S(1)}, u32[]{:S(2)}, u32[]{:S(2)}) collective-permute-start(bf16[128,16]{0,1:T(8,128)(2,1)S(1)} %collective-permute-done.7), channel_id=1, source_target_pairs={{0,27},{1,0},{2,1},{3,2},{8,3},{9,8},{10,9},{11,10},{16,11},{17,16... | collective-permute-start | bytes 12296 | tf_op jit(solution)/shard_map/ppermute | solution.py:29
  52.6 7.2 %collective-permute-start.10 = (bf16[128,16]{0,1:T(8,128)(2,1)S(1)}, bf16[128,16]{0,1:T(8,128)(2,1)S(1)}, u32[]{:S(2)}, u32[]{:S(2)}) collective-permute-start(bf16[128,16]{0,1:T(8,128)(2,1)S(1)} %collective-permute-done.8), channel_id=1, source_target_pairs={{0,1},{1,2},{2,3},{3,8},{8,9},{9,10},{10,11},{11,16},{16,17},{17,1... | collective-permute-start | bytes 12296 | tf_op jit(solution)/shard_map/ppermute | solution.py:26
  53.9 29.7 %collective-permute-start.11 = (bf16[128,16]{0,1:T(8,128)(2,1)S(1)}, bf16[128,16]{0,1:T(8,128)(2,1)S(1)}, u32[]{:S(2)}, u32[]{:S(2)}) collective-permute-start(bf16[128,16]{0,1:T(8,128)(2,1)S(1)} %collective-permute-done.9), channel_id=1, source_target_pairs={{0,27},{1,0},{2,1},{3,2},{8,3},{9,8},{10,9},{11,10},{16,11},{17,16... | collective-permute-start | bytes 12296 | tf_op jit(solution)/shard_map/ppermute | solution.py:29
  59.8 29.5 %collective-permute-start.12 = (bf16[128,16]{0,1:T(8,128)(2,1)S(1)}, bf16[128,16]{0,1:T(8,128)(2,1)S(1)}, u32[]{:S(2)}, u32[]{:S(2)}) collective-permute-start(bf16[128,16]{0,1:T(8,128)(2,1)S(1)} %collective-permute-done.10), channel_id=1, source_target_pairs={{0,1},{1,2},{2,3},{3,8},{8,9},{9,10},{10,11},{11,16},{16,17},{17,1... | collective-permute-start | bytes 12296 | tf_op jit(solution)/shard_map/ppermute | solution.py:26
  83.6 14.0 %collective-permute-start.13 = (bf16[128,16]{0,1:T(8,128)(2,1)S(1)}, bf16[128,16]{0,1:T(8,128)(2,1)S(1)}, u32[]{:S(2)}, u32[]{:S(2)}) collective-permute-start(bf16[128,16]{0,1:T(8,128)(2,1)S(1)} %collective-permute-done.11), channel_id=1, source_target_pairs={{0,27},{1,0},{2,1},{3,2},{8,3},{9,8},{10,9},{11,10},{16,11},{17,16... | collective-permute-start | bytes 12296 | tf_op jit(solution)/shard_map/ppermute | solution.py:29
  89.3 8.9 %collective-permute-start.14 = (bf16[128,16]{0,1:T(8,128)(2,1)S(1)}, bf16[128,16]{0,1:T(8,128)(2,1)S(1)}, u32[]{:S(2)}, u32[]{:S(2)}) collective-permute-start(bf16[128,16]{0,1:T(8,128)(2,1)S(1)} %collective-permute-done.12), channel_id=1, source_target_pairs={{0,1},{1,2},{2,3},{3,8},{8,9},{9,10},{10,11},{11,16},{16,17},{17,1... | collective-permute-start | bytes 12296 | tf_op jit(solution)/shard_map/ppermute | solution.py:26
  99.1 1.3 copy-start
  104.9 109.7 %reduce-scatter.12.cloned.1.call-start = ((), (), s32[]{:S(2)}) async-start(), calls=%async_computation.5 | async-start | bytes 139264
  105.8 142.5 %reduce-scatter.8.cloned.1.call-start = ((), (), s32[]{:S(2)}) async-start(), calls=%async_computation.3 | async-start | bytes 294912 | tf_op jit(solution)/shard_map/reduce_scatter | solution.py:59
Sparse Core Ops, SparseCore 0:
  105.1 32.1 reduce-scatter.9
  140.1 74.4 reduce-scatter.11
  218.2 29.9 reduce-scatter.7
